TPU v7x, 32 devices: a whole 2x2x4 slice. The times are simulated.
32 devices in a mesh: arc: 16 (over z, x, core), ord: 2 (over y).
Axes of the slice: x: 2, y: 2, z: 4, core: 2. Of those that a mesh axis runs over, the one named last changes fastest.
Arguments:
- design: bfloat16 [16384, 32768], P('arc', 'ord'), may hold values from -4 to 4
- arc_lengths: int32 [16], P('arc'), may hold values from 1 to 1024, 10240 in all
- kaula_prior: float32 [1024], replicated, may hold values from 1 to 20
Outputs:
- factor: float32 [1024, 32768], P('arc', 'ord')
Inputs may be any that keep to these rules, and one draw needn't show every extreme that they name: `arc_lengths`: some arc has all 1024 slots live.
All inputs are finite; a program needn't handle non-finite values. No bound on the sum of `arc_lengths` on one device may be relied on, other than what follows from the above.
Results may differ from a plain program's by a relative error of at most 0.0003.
Values may be sent and summed in bfloat16 or wider, within the bound.
A program may use at most 320 MiB of HBM per device.

v0:
```python
import math
import jax
import jax.numpy as jnp
from jax import lax
from jax.sharding import PartitionSpec as P

TILE = 512
PANELS = 2


def broadcast(block, axis, source):
    block = jnp.where(lax.axis_index(axis) == source, block, jnp.zeros_like(block))
    return lax.psum(block, axis)


def apply_panels(matrix, lowers, couplings):
    blocks = [matrix[p * TILE : (p + 1) * TILE] for p in range(PANELS)]
    for p in range(PANELS):
        blocks[p] = jax.scipy.linalg.solve_triangular(lowers[p], blocks[p], lower=True)
        for q in range(p + 1, PANELS):
            blocks[q] = blocks[q] - jnp.dot(
                couplings[p, q].T, blocks[p], precision=lax.Precision.HIGHEST
            )
    return jnp.concatenate(blocks, axis=0)


def on_device(design, arc_lengths, kaula_prior):
    obs_dev, ord_cols = design.shape
    arcs_here = arc_lengths.shape[0]
    arc_steps = obs_dev // arcs_here
    row_block = min(256, arc_steps)
    slab_rows = TILE * PANELS
    pieces = []
    for panel_index in range(PANELS):
        owner = panel_index * TILE // ord_cols
        offset = panel_index * TILE % ord_cols
        piece = design[:, offset : offset + TILE]
        pieces.append(broadcast(piece, "ord", owner))
    slab_cols = jnp.concatenate(pieces, axis=1)
    position = lax.broadcasted_iota(jnp.int32, (row_block, 1), 0)
    partial_value = jnp.zeros((slab_rows, ord_cols), jnp.float32)
    gram_part = jnp.zeros((slab_rows, slab_rows), jnp.float32)
    arc_slot = 0
    length = arc_lengths[arc_slot]
    blocks_live = (length + row_block - 1) // row_block

    def accumulate(step_idx, running, arc_slot=arc_slot, length=length):
        first_row = arc_slot * arc_steps + step_idx * row_block
        slab_block = lax.dynamic_slice_in_dim(slab_cols, first_row, row_block, 0)
        tile_block = lax.dynamic_slice_in_dim(design, first_row, row_block, 0)
        is_live = position + step_idx * row_block < length
        live_block = jnp.where(is_live, slab_block, jnp.zeros((), slab_block.dtype))
        dims = (((0,), (0,)), ((), ()))
        normal_acc = running[0] + lax.dot_general(
            live_block, tile_block, dims, preferred_element_type=jnp.float32
        )
        gram_acc = running[1] + lax.dot_general(
            live_block, slab_block, dims, preferred_element_type=jnp.float32
        )
        return (normal_acc, gram_acc)

    partial_value, gram_part = lax.fori_loop(0, blocks_live, accumulate, (partial_value, gram_part))
    inverse_norm = 1.0 / math.sqrt(lax.axis_size("arc") * obs_dev)
    square_ids = lax.broadcasted_iota(jnp.int32, (slab_rows, slab_rows), 0)
    square_cols = lax.broadcasted_iota(jnp.int32, (slab_rows, slab_rows), 1)
    gram = lax.psum(gram_part, "arc") * inverse_norm
    gram = gram + jnp.where(square_ids == square_cols, kaula_prior[:, None], 0.0)
    gram_blocks = [gram[p * TILE : (p + 1) * TILE] for p in range(PANELS)]
    lowers = []
    couplings = {}
    for p in range(PANELS):
        lower_factor = jnp.linalg.cholesky(gram_blocks[p][:, p * TILE : (p + 1) * TILE])
        lowers.append(lower_factor)
        gram_blocks[p] = jax.scipy.linalg.solve_triangular(lower_factor, gram_blocks[p], lower=True)
        for q in range(p + 1, PANELS):
            upper_tile = gram_blocks[p][:, q * TILE : (q + 1) * TILE]
            couplings[p, q] = upper_tile
            gram_blocks[q] = gram_blocks[q] - jnp.dot(
                upper_tile.T, gram_blocks[p], precision=lax.Precision.HIGHEST
            )
    row_index = lax.broadcasted_iota(jnp.int32, (slab_rows, 1), 0)
    summed = lax.psum_scatter(partial_value, "arc", scatter_dimension=1, tiled=True) * inverse_norm
    width = ord_cols // lax.axis_size("arc")
    col_first = lax.axis_index("ord") * ord_cols + lax.axis_index("arc") * width
    global_col = col_first + lax.broadcasted_iota(jnp.int32, (1, width), 1)
    matrix = summed + jnp.where(row_index == global_col, kaula_prior[:, None], 0.0)
    share = apply_panels(matrix, lowers, couplings)
    factor = lax.all_to_all(share, "arc", split_axis=0, concat_axis=1, tiled=True)
    return factor


def solution(mesh):
    in_specs = (P("arc", "ord"), P("arc"), P())
    out_specs = P("arc", "ord")
    return jax.shard_map(
        on_device, mesh=mesh, in_specs=in_specs, out_specs=out_specs, check_vma=False
    )
```

profile of v0, /device:TPU:1, one launch (start us, length us, event | category | flops | bytes accessed | tf_op | source)
XLA Modules:
  0.0 1504.7 jit_solution(2302760153561612100)
XLA Ops:
  6.5 3.0 slice_select_fusion.1
  10.3 64.6 %all-reduce.7.cloned.1.call-done = (bf16[1024,512]{1,0:T(8,128)(2,1)}, bf16[1024,512]{1,0:T(8,128)(2,1)}) async-done(((bf16[1024,512]{1,0:T(8,128)(2,1)}, bf16[1024,512]{1,0:T(8,128)(2,1)}), (bf16[1024,512]{1,0:T(8,128)(2,1)}, bf16[1024,512]{1,0:T(8,128)(2,1)})) %all-reduce.7.cloned.1.call-update) | async-done | bytes 2097168 | tf_op jit(solution)/shard_map/psum | solution.py:13
  76.7 21.0 %broadcast_in_dim.35 = f32[1024,16384]{1,0:T(8,128)} broadcast(f32[]{:T(128)} %constant.143.clone.1), dimensions={} | broadcast | bytes 67108864 | tf_op jit(solution)/shard_map/broadcast_in_dim | solution.py:41
  97.7 2.5 broadcast_in_dim.36.clone
  100.3 102.2 %while.19 = (s32[]{:T(128)}, f32[1024,16384]{1,0:T(8,128)}, f32[1024,1024]{1,0:T(8,128)}, s32[]{:T(128)}, s32[]{:T(128)}, /*index=5*/bf16[1024,1024]{1,0:T(8,128...) while((s32[]{:T(128)}, f32[1024,16384]{1,0:T(8,128)}, ...), condition=%wide.region_3.4_spmd.clone, body=%wide.region_2.3_spmd.clone.sunk | while | flops 9145156608 | bytes 152571312 | solution.py:62
  101.0 45.4 %convolution_add_fusion.4 = f32[1024,16384]{1,0:T(8,128)} fusion(f32[1024,16384]{1,0:T(8,128)} %get-tuple-element.287, bf16[1024,16384]{1,0:T(8,128)(2,1)} %get-tuple-element.303, s32[]{:T(128)S(6)} %select_n.66, pred[256]{0:T(512)(128)(4,1)S(1)} %compare_reduce_fusion.10, bf16[1024,1024]{1,0:T(8,128)(2,1)S(1)} %get-tuple-element.302), kind=kOutput, calls=%fused_computation.5.clone.3 | convolution fusion | flops 8606973952 | bytes 143132160 | tf_op jit(solution)/shard_map/while/body/dot_general | solution.py:54
  146.4 5.0 convolution_add_fusion.5
  152.1 45.4 %convolution_add_fusion.4 = f32[1024,16384]{1,0:T(8,128)} fusion(f32[1024,16384]{1,0:T(8,128)} %get-tuple-element.287, bf16[1024,16384]{1,0:T(8,128)(2,1)} %get-tuple-element.303, s32[]{:T(128)S(6)} %select_n.66, pred[256]{0:T(512)(128)(4,1)S(1)} %compare_reduce_fusion.10, bf16[1024,1024]{1,0:T(8,128)(2,1)S(1)} %get-tuple-element.302), kind=kOutput, calls=%fused_computation.5.clone.3 | convolution fusion | flops 8606973952 | bytes 143132160 | tf_op jit(solution)/shard_map/while/body/dot_general | solution.py:54
  197.5 5.0 convolution_add_fusion.5
  202.5 5.3 copy.13
  207.9 65.9 %copy.15 = f32[1024,16384]{0,1:T(8,128)} copy(f32[1024,16384]{1,0:T(8,128)} %get-tuple-element.52) | data formatting | bytes 134217728 | tf_op jit(solution)/shard_map/while | solution.py:62
  273.8 145.7 %all-reduce.5.cloned.1.call-done = f32[1024,1024]{0,1:T(8,128)} async-done(((f32[1024,1024]{0,1:T(8,128)}), f32[1024,1024]{0,1:T(8,128)}) %all-reduce.5.cloned.1.call-update) | async-done | bytes 4194320 | tf_op jit(solution)/shard_map/psum | solution.py:66
  419.5 641.4 %reduce-scatter.2.cloned.1.call-done = f32[1024,1024]{0,1:T(8,128)} async-done(((f32[1024,16384]{0,1:T(8,128)}), f32[1024,1024]{0,1:T(8,128)}) %reduce-scatter.2.cloned.1.call-update) | async-done | bytes 4194320 | tf_op jit(solution)/shard_map/reduce_scatter | solution.py:82
  1060.9 5.5 select_add_fusion.1
  1071.7 11.7 cholesky.286
  1083.6 9.8 custom-call.28
  1094.1 11.7 cholesky.305
  1105.8 10.3 custom-call.29
  1116.7 11.7 cholesky.326
  1129.1 9.8 custom-call.30
  1139.6 11.7 cholesky.343
  1155.5 7.8 while.20
  1163.3 39.3 %custom-call.31 = f32[4,128,128]{1,2,0:T(8,128)S(1)} custom-call(f32[4,128,128]{2,1,0:T(8,128)S(1)} %get-tuple-element.90), custom_call_target="InvertDiagBlocksLowerTriangular" | custom-call | tf_op jit(solution)/shard_map/jit(_solve_triangular)/triangular_solve | solution.py:19
  1204.3 2.0 convolution_subtract_fusion.4
  1207.0 2.9 convolution_subtract_fusion.1
  1210.5 3.8 fusion.54
  1215.0 3.5 fusion.23
  1222.9 11.7 cholesky.358
  1234.7 9.8 custom-call.33
  1247.8 11.7 cholesky.377
  1260.8 10.0 custom-call.34
  1273.9 13.2 cholesky.398
  1289.2 11.3 custom-call.35
  1302.8 11.7 cholesky.415
  1318.8 11.7 while.21
  1319.5 2.3 bitcast_dynamic-update-slice_fusion.5
  1322.4 2.3 bitcast_dynamic-update-slice_fusion.5
  1325.4 2.3 bitcast_dynamic-update-slice_fusion.5
  1328.3 2.2 bitcast_dynamic-update-slice_fusion.5
  1330.5 40.1 %custom-call.36 = f32[4,128,128]{1,2,0:T(8,128)} custom-call(f32[4,128,128]{2,1,0:T(8,128)S(1)} %get-tuple-element.92), custom_call_target="InvertDiagBlocksLowerTriangular" | custom-call | tf_op jit(solution)/shard_map/jit(_solve_triangular)/triangular_solve | solution.py:19
  1372.5 2.1 convolution_subtract_fusion.5
  1375.2 3.0 convolution_subtract_fusion.2
  1378.9 3.7 fusion.57
  1383.2 3.6 slice_subtract_fusion
  1390.2 2.7 convolution_subtract_fusion
  1393.6 3.7 fusion.51
  1398.7 96.8 %all_to_all.19 = f32[16,64,1024]{2,1,0:T(8,128)S(1)} all-to-all(f32[16,64,1024]{2,1,0:T(8,128)S(1)} %bitcast.117), channel_id=1, replica_groups=mesh['arc'=16,'ord'=2] {'arc'}, dimensions={0} | all-to-all | bytes 8388608 | tf_op jit(solution)/shard_map/all_to_all | solution.py:88
  1495.4 2.3 copy.32
  (108 shorter events, 54.5 us)
Async XLA Ops:
  6.5 68.4 %all-reduce.7.cloned.1.call-start = ((), (), s32[]{:S(2)}) async-start(), calls=%async_computation.4 | async-start | bytes 4194304 | tf_op jit(solution)/shard_map/psum | solution.py:13
  9.6 409.9 %all-reduce.5.cloned.1.call-start = ((), (), s32[]{:S(2)}) async-start(), calls=%async_computation.2 | async-start | bytes 8388608 | tf_op jit(solution)/shard_map/psum | solution.py:66
  207.9 853.0 %reduce-scatter.2.cloned.1.call-start = ((), (), s32[]{:S(2)}) async-start(), calls=%async_computation.3 | async-start | bytes 71303168 | tf_op jit(solution)/shard_map/reduce_scatter | solution.py:82
  273.8 787.1 %copy-start.7 = (f32[1024]{0:T(1024)S(1)}, f32[1024]{0:T(1024)}, u32[]{:S(2)}) copy-start(f32[1024]{0:T(1024)} %param.10) | copy-start | bytes 12292
  1066.4 1.9 copy-start
  1163.3 43.7 %copy-start.3 = (f32[512,512]{1,0:T(8,128)}, f32[512,512]{1,0:T(8,128)S(1)}, u32[]{:S(2)}) copy-start(f32[512,512]{1,0:T(8,128)S(1)} %get-tuple-element.346) | copy-start | bytes 3145732
  1214.3 4.2 copy-start.2
  1221.9 1.0 copy-start.4
  1247.1 0.7 copy-start.5
  1370.7 8.2 copy-start.1
  1383.2 3.6 copy-start.6
Sparse Core Ops, SparseCore 0:
  9.7 65.1 all-reduce.6
  208.0 211.4 all-reduce.4
  423.7 637.1 reduce-scatter.1
where the time goes:
time: 1510 us; the launch traced here: 1500 us
  waiting for transfers between devices  852 us (56%)
  other arithmetic  259 us (17%)
  matrix products  153 us (10%)
  local copies, waits for them, and re-layouts  124 us (8%)
  blocking collectives  96.8 us (6%)
  between operations  19.8 us (1%)
    reduce_scatter x1, waiting for transfers between devices, on_device(): lax.psum_scatter(partial_value, 'arc', scatter_dimension=1, tiled=True)  641 us
    another operation x29, other arithmetic, on_device(): jnp.linalg.cholesky(gram_blocks[p][:, p * TILE:(p + 1) * TILE])  163 us
    psum x1, waiting for transfers between devices, on_device(): gram = lax.psum(gram_part, 'arc') * inverse_norm  146 us
    all_to_all x1, blocking collectives, on_device(): lax.all_to_all(share, 'arc', split_axis=0, concat_axis=1, tiled=True)  96.8 us
    dot_general x2, matrix products, accumulate(): lax.dot_general(live_block, tile_block, dims, preferred_element_type=jnp....  90.8 us
    another operation x5, other arithmetic, apply_panels(): jax.scipy.linalg.solve_triangular(lowers[p], blocks[p], lower=True)  80.7 us
    while x2, local copies, waits for them, and re-layouts, on_device(): lax.fori_loop(0, blocks_live, accumulate, (partial_value, gram_part))  71.2 us
    psum x1, waiting for transfers between devices, broadcast(): return lax.psum(block, axis)  64.6 us
  transfers between devices with their start and end apart: 3, of which 3 were waited for; matrix products, arithmetic and copies ran while one was open for 4% of the time, Pallas kernels for 0%

commit v1 on v0

--- a/solution.py
+++ b/solution.py
@@ -85,7 +85,9 @@
     global_col = col_first + lax.broadcasted_iota(jnp.int32, (1, width), 1)
     matrix = summed + jnp.where(row_index == global_col, kaula_prior[:, None], 0.0)
     share = apply_panels(matrix, lowers, couplings)
-    factor = lax.all_to_all(share, "arc", split_axis=0, concat_axis=1, tiled=True)
+    z_new = jnp.stack(jnp.split(share, lax.axis_size("arc"), 0), axis=0)
+    piece_next = lax.all_to_all(z_new, "arc", 0, 0)
+    factor = jnp.concatenate(piece_next, 1)
     return factor
 
 

time: 1510 us -> 1520 us (level)
  no operation moved by 1% of the time
where the time goes in v1:
time: 1520 us; the launch traced here: 1510 us
  waiting for transfers between devices  852 us (56%)
  other arithmetic  258 us (17%)
  matrix products  155 us (10%)
  local copies, waits for them, and re-layouts  126 us (8%)
  blocking collectives  96.8 us (6%)
  between operations  20 us (1%)
    reduce_scatter x1, waiting for transfers between devices, on_device(): lax.psum_scatter(partial_value, 'arc', scatter_dimension=1, tiled=True)  641 us
    another operation x29, other arithmetic, on_device(): jnp.linalg.cholesky(gram_blocks[p][:, p * TILE:(p + 1) * TILE])  163 us
    psum x1, waiting for transfers between devices, on_device(): gram = lax.psum(gram_part, 'arc') * inverse_norm  146 us
    all_to_all x1, blocking collectives, on_device(): piece_next = lax.all_to_all(z_new, 'arc', 0, 0)  96.8 us
    dot_general x2, matrix products, accumulate(): lax.dot_general(live_block, tile_block, dims, preferred_element_type=jnp....  90.8 us
    another operation x5, other arithmetic, apply_panels(): jax.scipy.linalg.solve_triangular(lowers[p], blocks[p], lower=True)  80.5 us
    while x2, local copies, waits for them, and re-layouts, on_device(): lax.fori_loop(0, blocks_live, accumulate, (partial_value, gram_part))  71.2 us
    psum x1, waiting for transfers between devices, broadcast(): return lax.psum(block, axis)  64.6 us
  transfers between devices with their start and end apart: 3, of which 3 were waited for; matrix products, arithmetic and copies ran while one was open for 4% of the time, Pallas kernels for 0%

profile of v1, /device:TPU:1, one launch (start us, length us, event | category | flops | bytes accessed | tf_op | source)
XLA Modules:
  0.0 1508.5 jit_solution(1405300804076293923)
XLA Ops:
  6.5 3.0 slice_select_fusion.1
  10.3 64.6 %all-reduce.7.cloned.1.call-done = (bf16[1024,512]{1,0:T(8,128)(2,1)}, bf16[1024,512]{1,0:T(8,128)(2,1)}) async-done(((bf16[1024,512]{1,0:T(8,128)(2,1)}, bf16[1024,512]{1,0:T(8,128)(2,1)}), (bf16[1024,512]{1,0:T(8,128)(2,1)}, bf16[1024,512]{1,0:T(8,128)(2,1)})) %all-reduce.7.cloned.1.call-update) | async-done | bytes 2097168 | tf_op jit(solution)/shard_map/psum | solution.py:13
  76.7 21.0 %broadcast_in_dim.35 = f32[1024,16384]{1,0:T(8,128)} broadcast(f32[]{:T(128)} %constant.143.clone.1), dimensions={} | broadcast | bytes 67108864 | tf_op jit(solution)/shard_map/broadcast_in_dim | solution.py:41
  97.7 2.5 broadcast_in_dim.36.clone
  100.3 102.2 %while.19 = (s32[]{:T(128)}, f32[1024,16384]{1,0:T(8,128)}, f32[1024,1024]{1,0:T(8,128)}, s32[]{:T(128)}, s32[]{:T(128)}, /*index=5*/bf16[1024,1024]{1,0:T(8,128...) while((s32[]{:T(128)}, f32[1024,16384]{1,0:T(8,128)}, ...), condition=%wide.region_3.4_spmd.clone, body=%wide.region_2.3_spmd.clone.sunk | while | flops 9145156608 | bytes 152571312 | solution.py:62
  101.0 45.4 %convolution_add_fusion.4 = f32[1024,16384]{1,0:T(8,128)} fusion(f32[1024,16384]{1,0:T(8,128)} %get-tuple-element.287, bf16[1024,16384]{1,0:T(8,128)(2,1)} %get-tuple-element.303, s32[]{:T(128)S(6)} %select_n.66, pred[256]{0:T(512)(128)(4,1)S(1)} %compare_reduce_fusion.10, bf16[1024,1024]{1,0:T(8,128)(2,1)S(1)} %get-tuple-element.302), kind=kOutput, calls=%fused_computation.5.clone.3 | convolution fusion | flops 8606973952 | bytes 143132160 | tf_op jit(solution)/shard_map/while/body/dot_general | solution.py:54
  146.4 5.0 convolution_add_fusion.5
  152.1 45.4 %convolution_add_fusion.4 = f32[1024,16384]{1,0:T(8,128)} fusion(f32[1024,16384]{1,0:T(8,128)} %get-tuple-element.287, bf16[1024,16384]{1,0:T(8,128)(2,1)} %get-tuple-element.303, s32[]{:T(128)S(6)} %select_n.66, pred[256]{0:T(512)(128)(4,1)S(1)} %compare_reduce_fusion.10, bf16[1024,1024]{1,0:T(8,128)(2,1)S(1)} %get-tuple-element.302), kind=kOutput, calls=%fused_computation.5.clone.3 | convolution fusion | flops 8606973952 | bytes 143132160 | tf_op jit(solution)/shard_map/while/body/dot_general | solution.py:54
  197.5 5.0 convolution_add_fusion.5
  202.5 5.3 copy.12
  207.9 65.9 %copy.14 = f32[1024,16384]{0,1:T(8,128)} copy(f32[1024,16384]{1,0:T(8,128)} %get-tuple-element.52) | data formatting | bytes 134217728 | tf_op jit(solution)/shard_map/while | solution.py:62
  273.8 145.7 %all-reduce.5.cloned.1.call-done = f32[1024,1024]{0,1:T(8,128)} async-done(((f32[1024,1024]{0,1:T(8,128)}), f32[1024,1024]{0,1:T(8,128)}) %all-reduce.5.cloned.1.call-update) | async-done | bytes 4194320 | tf_op jit(solution)/shard_map/psum | solution.py:66
  419.5 641.4 %reduce-scatter.2.cloned.1.call-done = f32[1024,1024]{0,1:T(8,128)} async-done(((f32[1024,16384]{0,1:T(8,128)}), f32[1024,1024]{0,1:T(8,128)}) %reduce-scatter.2.cloned.1.call-update) | async-done | bytes 4194320 | tf_op jit(solution)/shard_map/reduce_scatter | solution.py:82
  1060.9 5.5 select_add_fusion.1
  1071.8 11.7 cholesky.286
  1083.7 9.8 custom-call.28
  1094.2 11.7 cholesky.305
  1105.9 10.3 custom-call.29
  1116.9 11.7 cholesky.326
  1129.3 9.8 custom-call.30
  1139.7 11.7 cholesky.343
  1155.7 8.1 while.20
  1163.9 39.3 %custom-call.31 = f32[4,128,128]{1,2,0:T(8,128)S(1)} custom-call(f32[4,128,128]{2,1,0:T(8,128)S(1)} %get-tuple-element.90), custom_call_target="InvertDiagBlocksLowerTriangular" | custom-call | tf_op jit(solution)/shard_map/jit(_solve_triangular)/triangular_solve | solution.py:19
  1206.6 2.8 convolution_subtract_fusion.5
  1210.1 2.0 convolution_subtract_fusion.4
  1212.8 2.9 convolution_subtract_fusion.1
  1216.3 3.7 fusion.54
  1221.5 3.9 fusion.15
  1229.4 11.7 cholesky.358
  1241.3 9.8 custom-call.33
  1254.3 11.9 cholesky.377
  1267.6 9.8 custom-call.34
  1280.4 13.2 cholesky.398
  1295.8 11.3 custom-call.35
  1309.4 11.9 cholesky.415
  1325.6 11.7 while.21
  1326.3 2.2 bitcast_dynamic-update-slice_fusion.5
  1329.2 2.2 bitcast_dynamic-update-slice_fusion.5
  1332.2 2.2 bitcast_dynamic-update-slice_fusion.5
  1335.1 2.2 bitcast_dynamic-update-slice_fusion.5
  1337.3 39.9 %custom-call.36 = f32[4,128,128]{1,2,0:T(8,128)} custom-call(f32[4,128,128]{2,1,0:T(8,128)S(1)} %get-tuple-element.92), custom_call_target="InvertDiagBlocksLowerTriangular" | custom-call | tf_op jit(solution)/shard_map/jit(_solve_triangular)/triangular_solve | solution.py:19
  1379.1 2.9 convolution_subtract_fusion.2
  1382.7 3.7 fusion.57
  1387.0 3.6 slice_subtract_fusion
  1394.1 3.0 convolution_subtract_fusion
  1397.8 3.6 fusion.51
  1402.5 96.8 %all_to_all.5 = f32[16,64,1024]{2,1,0:T(8,128)S(1)} all-to-all(f32[16,64,1024]{2,1,0:T(8,128)S(1)} %fusion.77), channel_id=1, replica_groups=mesh['arc'=16,'ord'=2] {'arc'}, dimensions={0} | all-to-all | bytes 8388608 | tf_op jit(solution)/shard_map/all_to_all | solution.py:89
  1499.2 2.3 copy.31
  (129 shorter events, 56.9 us)
Async XLA Ops:
  6.5 68.4 %all-reduce.7.cloned.1.call-start = ((), (), s32[]{:S(2)}) async-start(), calls=%async_computation.4 | async-start | bytes 4194304 | tf_op jit(solution)/shard_map/psum | solution.py:13
  9.6 409.9 %all-reduce.5.cloned.1.call-start = ((), (), s32[]{:S(2)}) async-start(), calls=%async_computation.2 | async-start | bytes 8388608 | tf_op jit(solution)/shard_map/psum | solution.py:66
  207.9 853.0 %reduce-scatter.2.cloned.1.call-start = ((), (), s32[]{:S(2)}) async-start(), calls=%async_computation.3 | async-start | bytes 71303168 | tf_op jit(solution)/shard_map/reduce_scatter | solution.py:82
  273.8 787.1 %copy-start.10 = (f32[1024]{0:T(1024)S(1)}, f32[1024]{0:T(1024)}, u32[]{:S(2)}) copy-start(f32[1024]{0:T(1024)} %param.10) | copy-start | bytes 12292
  1066.4 2.0 copy-start
  1163.8 52.5 %copy-start.4 = (f32[512,512]{1,0:T(8,128)}, f32[512,512]{1,0:T(8,128)S(1)}, u32[]{:S(2)}) copy-start(f32[512,512]{1,0:T(8,128)S(1)} %get-tuple-element.346) | copy-start | bytes 3145732
  1220.0 5.4 copy-start.3
  1220.7 0.8 copy-start.6
  1228.4 1.0 copy-start.5
  1253.6 0.7 copy-start.8
  1377.2 5.4 copy-start.1
  1377.2 9.8 copy-start.7
  1387.0 3.6 copy-start.9
  1393.1 8.9 copy-start.2
Sparse Core Ops, SparseCore 0:
  9.7 65.1 all-reduce.6
  208.0 211.4 all-reduce.4
  423.7 637.1 reduce-scatter.1
